TPU v7x, 32 devices: a whole 2x2x4 slice. The times are simulated.
32 devices in a mesh: ctx: 4 (over z), fsdp: 8 (over y, x, core).
Axes of the slice: x: 2, y: 2, z: 4, core: 2. Of those that a mesh axis runs over, the one named last changes fastest.
Arguments:
- tokens: bfloat16 [8, 1024, 2048], P('fsdp', 'ctx'), may hold values from -6 to 6
- attn_gain: bfloat16 [2048], P('fsdp'), may hold values from 0.25 to 1.75
- w_query: bfloat16 [2048, 2048], P('fsdp'), may hold values from -1.2374369 to 1.2374369
- w_key: bfloat16 [2048, 256], P('fsdp'), may hold values from -0.13258252 to 0.13258252
- w_value: bfloat16 [2048, 256], P('fsdp'), may hold values from -0.125 to 0.125
- w_out: bfloat16 [2048, 2048], P('fsdp'), may hold values from -1.5 to 1.5
- ffn_gain: bfloat16 [2048], P('fsdp'), may hold values from 0.25 to 1.75
- w_gate: bfloat16 [2048, 5632], P('fsdp'), may hold values from -0.125 to 0.125
- w_up: bfloat16 [2048, 5632], P('fsdp'), may hold values from -0.125 to 0.125
- w_down: bfloat16 [5632, 2048], P('fsdp'), may hold values from -0.078125 to 0.078125
- block_table: int32 [4, 2], replicated, may hold values from 0 to 7, as said below
- positions: int32 [8, 1024], P('fsdp', 'ctx'), may hold values from 0 to 5118, as said below
- out_grad: bfloat16 [8, 1024, 2048], P('fsdp', 'ctx'), may hold values from -6 to 6
Outputs:
- layer_out: bfloat16 [8, 1024, 2048], P('fsdp', 'ctx')
- tokens_grad: float32 [8, 1024, 2048], P('fsdp', 'ctx')
- attn_gain_grad: float32 [2048], P('fsdp')
- w_query_grad: float32 [2048, 2048], P('fsdp')
- w_key_grad: float32 [2048, 256], P('fsdp')
- w_value_grad: float32 [2048, 256], P('fsdp')
- w_out_grad: float32 [2048, 2048], P('fsdp')
- ffn_gain_grad: float32 [2048], P('fsdp')
- w_gate_grad: float32 [2048, 5632], P('fsdp')
- w_up_grad: float32 [2048, 5632], P('fsdp')
- w_down_grad: float32 [5632, 2048], P('fsdp')
Inputs may be any that keep to these rules, and one draw needn't show every extreme that they name: `block_table`: row c holds a block p and its mirror 8 - 1 - p; every block of 0 to 7 stands once in the table. positions[s, r] is an offset of sequence s plus idx of stored row r, so positions rise by one along a sequence.
All inputs are finite; a program needn't handle non-finite values.
Results may differ from a plain program's by a relative error of at most 0.014.
Values may be sent and summed in bfloat16 or wider, within the bound.
A program may use at most 512 MiB of HBM per device.

v0:
```python
import jax
import jax.numpy as jnp
from jax import lax
from jax.sharding import PartitionSpec as P

HEADS = 32
KV_HEADS = 4
HEAD_DIM = 64
EPS = 1e-05
THETA = 10000.0


def rope_tables(positions):
    half_dim = HEAD_DIM // 2
    frequency = THETA ** (-jnp.arange(half_dim, dtype=jnp.float32) * (2.0 / HEAD_DIM))
    angle = positions.astype(jnp.float32)[:, None] * frequency[None, :]
    return (jnp.cos(angle)[:, None, :], jnp.sin(angle)[:, None, :])


def rotate(values, cosine, sine):
    half_dim = HEAD_DIM // 2
    first = values[..., :half_dim]
    second = values[..., half_dim:]
    return jnp.concatenate(
        [first * cosine - second * sine, second * cosine + first * sine], axis=-1
    )


def unrotate(grads, cosine, sine):
    half_dim = HEAD_DIM // 2
    first = grads[..., :half_dim]
    second = grads[..., half_dim:]
    return jnp.concatenate(
        [first * cosine + second * sine, second * cosine - first * sine], axis=-1
    )


def contract_rows(left, right):
    return lax.dot_general(
        left, right, (((0,), (0,)), ((), ())), preferred_element_type=jnp.float32
    )


def times_transpose(left, right):
    return lax.dot_general(
        left, right, (((1,), (1,)), ((), ())), preferred_element_type=jnp.float32
    )


def shards(
    tokens,
    attn_gain,
    w_query,
    w_key,
    w_value,
    w_out,
    ffn_gain,
    w_gate,
    w_up,
    w_down,
    block_table,
    positions,
    out_grad,
):
    inputs = tokens[0].astype(jnp.float32)
    cotangent = out_grad[0].astype(jnp.float32)
    local_rows = inputs.shape[0]
    model_width = inputs.shape[1]
    hidden_width = w_gate.shape[1]
    group_size = HEADS // KV_HEADS
    query_width = HEADS * HEAD_DIM
    key_width = KV_HEADS * HEAD_DIM
    score_scale = HEAD_DIM ** (-0.5)
    cosine, sine = rope_tables(positions[0])
    block_rows = local_rows // 2
    seq_index = (
        block_table[:, :, None] * block_rows
        + jnp.arange(block_rows, dtype=jnp.int32)[None, None, :]
    ).reshape(-1)
    own_index = lax.dynamic_slice_in_dim(seq_index, lax.axis_index("ctx") * local_rows, local_rows)
    allowed = seq_index[None, :] <= own_index[:, None]
    inverse_one = lax.rsqrt(jnp.mean(inputs * inputs, axis=1, keepdims=True) + EPS)
    unit_one = inputs * inverse_one
    gain_piece = lax.all_gather(attn_gain, "fsdp", axis=0, tiled=True)
    query_piece = lax.all_gather(w_query, "fsdp", axis=0, tiled=True)
    key_piece = lax.all_gather(w_key, "fsdp", axis=0, tiled=True)
    value_piece = lax.all_gather(w_value, "fsdp", axis=0, tiled=True)
    out_piece = lax.all_gather(w_out, "fsdp", axis=0, tiled=True)
    columns = (unit_one * gain_piece.astype(jnp.float32)[None, :]).astype(jnp.bfloat16)
    query_sum = jnp.dot(columns, query_piece, preferred_element_type=jnp.float32)
    key_sum = jnp.dot(columns, key_piece, preferred_element_type=jnp.float32)
    value_sum = jnp.dot(columns, value_piece, preferred_element_type=jnp.float32)
    normed = columns
    out_full = out_piece
    query_sum, key_sum, value_sum, normed_one, out_full = (
        query_sum,
        key_sum,
        value_sum,
        normed,
        out_full,
    )
    queries_low = rotate(query_sum.reshape(local_rows, HEADS, HEAD_DIM), cosine, sine).astype(
        jnp.bfloat16
    )
    keys_low = (
        rotate(key_sum.reshape(local_rows, KV_HEADS, HEAD_DIM), cosine, sine)
        .reshape(local_rows, key_width)
        .astype(jnp.bfloat16)
    )
    values_low = value_sum.astype(jnp.bfloat16)
    keys_all, values_all = (
        lax.all_gather(keys_low, "ctx", axis=0, tiled=True),
        lax.all_gather(values_low, "ctx", axis=0, tiled=True),
    )
    seq_length = keys_all.shape[0]
    query_heads = queries_low.reshape(local_rows, KV_HEADS, group_size, HEAD_DIM).transpose(
        1, 2, 0, 3
    )
    key_heads = keys_all.reshape(seq_length, KV_HEADS, HEAD_DIM).transpose(1, 0, 2)
    value_heads = values_all.reshape(seq_length, KV_HEADS, HEAD_DIM).transpose(1, 0, 2)

    def scores_of(query_one, key_block):
        raw = times_transpose(query_one, key_block) * score_scale
        return jnp.where(allowed, raw, -1e30)

    def head_forward(operands):
        query_block, key_block, value_block = operands

        def single(query_one):
            scores = scores_of(query_one, key_block)
            highest = jnp.max(scores, axis=-1, keepdims=True)
            weights = jnp.exp(scores - highest)
            totals = jnp.sum(weights, axis=-1, keepdims=True)
            softmaxed = (weights / totals).astype(jnp.bfloat16)
            mixed = jnp.dot(softmaxed, value_block, preferred_element_type=jnp.float32)
            return (mixed, highest[:, 0] + jnp.log(totals[:, 0]))

        return lax.map(single, query_block)

    mixed_heads, log_totals = lax.map(head_forward, (query_heads, key_heads, value_heads))
    attended = (
        mixed_heads.transpose(2, 0, 1, 3).reshape(local_rows, query_width).astype(jnp.bfloat16)
    )
    hidden_one = inputs + jnp.dot(attended, out_full, preferred_element_type=jnp.float32)
    inverse_two = lax.rsqrt(jnp.mean(hidden_one * hidden_one, axis=1, keepdims=True) + EPS)
    unit_two = hidden_one * inverse_two
    gain_piece = lax.all_gather(ffn_gain, "fsdp", axis=0, tiled=True)
    gate_piece = lax.all_gather(w_gate, "fsdp", axis=0, tiled=True)
    up_piece = lax.all_gather(w_up, "fsdp", axis=0, tiled=True)
    columns = (unit_two * gain_piece.astype(jnp.float32)[None, :]).astype(jnp.bfloat16)
    gate_sum = jnp.dot(columns, gate_piece, preferred_element_type=jnp.float32)
    up_sum = jnp.dot(columns, up_piece, preferred_element_type=jnp.float32)
    sigmoid_gate = jax.nn.sigmoid(gate_sum)
    silu_gate = gate_sum * sigmoid_gate
    activated = (silu_gate * up_sum).astype(jnp.bfloat16)
    branch_out = jnp.dot(
        activated,
        lax.all_gather(w_down, "fsdp", axis=0, tiled=True),
        preferred_element_type=jnp.float32,
    )
    layer_out = (hidden_one + branch_out).astype(jnp.bfloat16)
    grad_branch = cotangent.astype(jnp.bfloat16)
    grad_activated = times_transpose(
        grad_branch, lax.all_gather(w_down, "fsdp", axis=0, tiled=True)
    )
    grad_gate = (
        grad_activated * up_sum * sigmoid_gate * (1.0 + gate_sum * (1.0 - sigmoid_gate))
    ).astype(jnp.bfloat16)
    grad_up = (grad_activated * silu_gate).astype(jnp.bfloat16)
    gain_piece = lax.all_gather(ffn_gain, "fsdp", axis=0, tiled=True)
    gate_piece = lax.all_gather(w_gate, "fsdp", axis=0, tiled=True)
    up_piece = lax.all_gather(w_up, "fsdp", axis=0, tiled=True)
    grad_cols = times_transpose(grad_gate, gate_piece) + times_transpose(grad_up, up_piece)
    gain_grad = jnp.sum(grad_cols * unit_two, axis=0)
    grad_unit = grad_cols * gain_piece.astype(jnp.float32)[None, :]
    grad_unit_two = grad_unit
    gain_grad_two = gain_grad
    grad_gate_up = jnp.concatenate([grad_gate, grad_up], axis=1)
    down_shard = lax.psum_scatter(
        contract_rows(activated, grad_branch), "fsdp", scatter_dimension=0, tiled=True
    )
    gate_up_shard = lax.psum_scatter(
        contract_rows(columns, grad_gate_up), "fsdp", scatter_dimension=0, tiled=True
    )
    grad_hidden = cotangent + inverse_two * (
        grad_unit_two - unit_two * jnp.mean(grad_unit_two * unit_two, axis=1, keepdims=True)
    )
    grad_attn_low = grad_hidden.astype(jnp.bfloat16)
    grad_attended = times_transpose(
        grad_attn_low, lax.all_gather(w_out, "fsdp", axis=0, tiled=True)
    ).astype(jnp.bfloat16)
    out_term = contract_rows(attended, grad_attn_low)
    grad_heads = grad_attended.reshape(local_rows, KV_HEADS, group_size, HEAD_DIM).transpose(
        1, 2, 0, 3
    )

    def head_backward(operands):
        query_block, key_block, value_block, grad_block, log_block = operands

        def single(carry, items):
            key_total, value_total = carry
            query_one, grad_one, log_one = items
            scores = scores_of(query_one, key_block)
            softmaxed = jnp.exp(scores - log_one[:, None])
            grad_probs = times_transpose(grad_one, value_block)
            inner = jnp.sum(softmaxed * grad_probs, axis=-1, keepdims=True)
            grad_scores = (softmaxed * (grad_probs - inner)).astype(jnp.bfloat16)
            grad_query = (
                jnp.dot(grad_scores, key_block, preferred_element_type=jnp.float32) * score_scale
            )
            key_total = key_total + contract_rows(grad_scores, query_one) * score_scale
            value_total = value_total + contract_rows(softmaxed.astype(jnp.bfloat16), grad_one)
            return ((key_total, value_total), grad_query)

        start_totals = (
            jnp.zeros((seq_length, HEAD_DIM), jnp.float32),
            jnp.zeros((seq_length, HEAD_DIM), jnp.float32),
        )
        (key_total, value_total), grad_query = lax.scan(
            single, start_totals, (query_block, grad_block, log_block)
        )
        return (grad_query, key_total, value_total)

    grad_query_heads, grad_key_heads, grad_value_heads = lax.map(
        head_backward, (query_heads, key_heads, value_heads, grad_heads, log_totals)
    )
    grad_keys_all = grad_key_heads.transpose(1, 0, 2).reshape(seq_length, key_width)
    grad_values_all = grad_value_heads.transpose(1, 0, 2).reshape(seq_length, key_width)
    own_key_grad, own_value_grad = (
        lax.psum_scatter(grad_keys_all, "ctx", scatter_dimension=0, tiled=True),
        lax.psum_scatter(grad_values_all, "ctx", scatter_dimension=0, tiled=True),
    )
    grad_key_low = (
        unrotate(own_key_grad.reshape(local_rows, KV_HEADS, HEAD_DIM), cosine, sine)
        .reshape(local_rows, key_width)
        .astype(jnp.bfloat16)
    )
    grad_value_low = own_value_grad.astype(jnp.bfloat16)
    grad_query_rows = grad_query_heads.transpose(2, 0, 1, 3).reshape(local_rows, HEADS, HEAD_DIM)
    grad_query_low = (
        unrotate(grad_query_rows, cosine, sine)
        .reshape(local_rows, query_width)
        .astype(jnp.bfloat16)
    )
    gain_piece = lax.all_gather(attn_gain, "fsdp", axis=0, tiled=True)
    query_piece = lax.all_gather(w_query, "fsdp", axis=0, tiled=True)
    key_piece = lax.all_gather(w_key, "fsdp", axis=0, tiled=True)
    value_piece = lax.all_gather(w_value, "fsdp", axis=0, tiled=True)
    grad_cols = (
        times_transpose(grad_query_low, query_piece)
        + times_transpose(grad_key_low, key_piece)
        + times_transpose(grad_value_low, value_piece)
    )
    gain_grad = jnp.sum(grad_cols * unit_one, axis=0)
    grad_unit = grad_cols * gain_piece.astype(jnp.float32)[None, :]
    tokens_grad = grad_hidden + inverse_one * (
        grad_unit - unit_one * jnp.mean(grad_unit * unit_one, axis=1, keepdims=True)
    )
    query_term = contract_rows(normed_one, grad_query_low)
    key_term = contract_rows(normed_one, grad_key_low)
    value_term = contract_rows(normed_one, grad_value_low)
    gain_one_shard, gain_two_shard, query_shard, key_shard, value_shard, out_shard = (
        lax.psum_scatter(gain_grad, "fsdp", scatter_dimension=0, tiled=True),
        lax.psum_scatter(gain_grad_two, "fsdp", scatter_dimension=0, tiled=True),
        lax.psum_scatter(query_term, "fsdp", scatter_dimension=0, tiled=True),
        lax.psum_scatter(key_term, "fsdp", scatter_dimension=0, tiled=True),
        lax.psum_scatter(value_term, "fsdp", scatter_dimension=0, tiled=True),
        lax.psum_scatter(out_term, "fsdp", scatter_dimension=0, tiled=True),
    )
    gate_shard = gate_up_shard[:, :hidden_width]
    up_shard = gate_up_shard[:, hidden_width:]
    summed = lax.psum(
        (
            gain_one_shard,
            query_shard,
            key_shard,
            value_shard,
            out_shard,
            gain_two_shard,
            gate_shard,
            up_shard,
            down_shard,
        ),
        "ctx",
    )
    return (
        layer_out.reshape(1, local_rows, model_width),
        tokens_grad.reshape(1, local_rows, model_width),
        summed[0],
        summed[1],
        summed[2],
        summed[3],
        summed[4],
        summed[5],
        summed[6],
        summed[7],
        summed[8],
    )


def solution(mesh):
    return jax.shard_map(
        shards,
        mesh=mesh,
        in_specs=(
            P("fsdp", "ctx", None),
            P("fsdp"),
            P("fsdp", None),
            P("fsdp", None),
            P("fsdp", None),
            P("fsdp", None),
            P("fsdp"),
            P("fsdp", None),
            P("fsdp", None),
            P("fsdp", None),
            P(),
            P("fsdp", "ctx"),
            P("fsdp", "ctx", None),
        ),
        out_specs=(
            P("fsdp", "ctx", None),
            P("fsdp", "ctx", None),
            P("fsdp"),
            P("fsdp", None),
            P("fsdp", None),
            P("fsdp", None),
            P("fsdp", None),
            P("fsdp"),
            P("fsdp", None),
            P("fsdp", None),
            P("fsdp", None),
        ),
        check_vma=False,
    )
```

profile of v0, /device:TPU:0, one launch (start us, length us, event | category | flops | bytes accessed | tf_op | source)
XLA Modules:
  0.0 3205.1 jit_solution(12606878503554546676)
XLA Ops:
  38.3 16.1 all_gather.45
  63.3 16.6 all_gather.47
  81.4 36.5 %all-gather.10.cloned.1.call-done = bf16[2048,2048]{1,0:T(8,128)(2,1)} async-done(((bf16[256,2048]{1,0:T(8,128)(2,1)}), bf16[2048,2048]{1,0:T(8,128)(2,1)}) %all-gather.10.cloned.1.call-update) | async-done | bytes 8388624 | tf_op jit(solution)/shard_map/all_gather | solution.py:85
  117.9 12.3 copy.43
  144.6 60.9 %while.64 = (s32[]{:T(128)}, bf16[4,8,256,64]{2,3,1,0:T(8,128)(2,1)}, f32[4,8,256]{2,1,0:T(8,128)S(1)}, bf16[4,8,256,64]{3,2,1,0:T(8,128)(2,1)}, bf16[4,1024,64]...) while((s32[]{:T(128)}, ...), condition=%wide.region_6.7_spmd.clone.clone, body=%wide.region_1.6_spmd.clone.sunk.clone | while | flops 69467904 | bytes 6454618 | solution.py:140
  178.1 11.6 while.63
  212.9 79.4 %all-gather.18.cloned.1.call-done = bf16[2048,5632]{1,0:T(8,128)(2,1)} async-done(((bf16[256,5632]{1,0:T(8,128)(2,1)}), bf16[2048,5632]{1,0:T(8,128)(2,1)}) %all-gather.18.cloned.1.call-update) | async-done | bytes 23068688 | tf_op jit(solution)/shard_map/all_gather | solution.py:148
  292.4 13.5 fusion.81
  305.8 104.8 %all-gather.20.cloned.1.call-done = bf16[2048,5632]{1,0:T(8,128)(2,1)} async-done(((bf16[256,5632]{1,0:T(8,128)(2,1)}), bf16[2048,5632]{1,0:T(8,128)(2,1)}) %all-gather.20.cloned.1.call-update) | async-done | bytes 23068688 | tf_op jit(solution)/shard_map/all_gather | solution.py:149
  410.6 13.6 fusion.82
  424.2 104.7 %all-gather.22.cloned.1.call-done = bf16[5632,2048]{1,0:T(8,128)(2,1)} async-done(((bf16[704,2048]{1,0:T(8,128)(2,1)}), bf16[5632,2048]{1,0:T(8,128)(2,1)}) %all-gather.22.cloned.1.call-update) | async-done | bytes 23068688 | tf_op jit(solution)/shard_map/all_gather | solution.py:158
  529.0 18.5 multiply_convert_fusion.1
  547.5 12.5 fusion.83
  560.0 14.0 multiply_reduce_fusion.1
  583.8 168.1 %while.66 = (s32[]{:T(128)}, f32[4,8,256,64]{2,3,1,0:T(8,128)}, f32[4,1024,64]{1,2,0:T(8,128)}, f32[4,1024,64]{1,2,0:T(8,128)}, bf16[4,8,256,64]{3,2,1,0:T(8,128...) while((s32[]{:T(128)}, f32[4,8,256,64]{2,3,1,0:T(8,128)}, ...), condition=%wide.region_13.14_spmd.clone.clone, body=%wide.region_9.13_spmd.clone.sunk.clone | while | flops 170737408 | bytes 22899168 | solution.py:224
  588.6 34.4 %while.65 = (s32[]{:T(128)}, f32[1024,64]{0,1:T(8,128)S(1)}, f32[1024,64]{0,1:T(8,128)S(1)}, f32[8,256,64]{1,2,0:T(8,128)}, bf16[8,256,64]{2,1,0:T(8,128)(2,1)},...) while((s32[]{:T(128)}, f32[1024,64]{0,1:T(8,128)S(1)}, ...), condition=%wide.region_12.12_spmd.clone, body=%wide.region_10.11_spmd.clone.sunk | while | flops 170475264 | bytes 10032288 | solution.py:219
  630.6 34.4 %while.65 = (s32[]{:T(128)}, f32[1024,64]{0,1:T(8,128)S(1)}, f32[1024,64]{0,1:T(8,128)S(1)}, f32[8,256,64]{1,2,0:T(8,128)}, bf16[8,256,64]{2,1,0:T(8,128)(2,1)},...) while((s32[]{:T(128)}, f32[1024,64]{0,1:T(8,128)S(1)}, ...), condition=%wide.region_12.12_spmd.clone, body=%wide.region_10.11_spmd.clone.sunk | while | flops 170475264 | bytes 10032288 | solution.py:219
  672.6 34.4 %while.65 = (s32[]{:T(128)}, f32[1024,64]{0,1:T(8,128)S(1)}, f32[1024,64]{0,1:T(8,128)S(1)}, f32[8,256,64]{1,2,0:T(8,128)}, bf16[8,256,64]{2,1,0:T(8,128)(2,1)},...) while((s32[]{:T(128)}, f32[1024,64]{0,1:T(8,128)S(1)}, ...), condition=%wide.region_12.12_spmd.clone, body=%wide.region_10.11_spmd.clone.sunk | while | flops 170475264 | bytes 10032288 | solution.py:219
  714.6 34.4 %while.65 = (s32[]{:T(128)}, f32[1024,64]{0,1:T(8,128)S(1)}, f32[1024,64]{0,1:T(8,128)S(1)}, f32[8,256,64]{1,2,0:T(8,128)}, bf16[8,256,64]{2,1,0:T(8,128)(2,1)},...) while((s32[]{:T(128)}, f32[1024,64]{0,1:T(8,128)S(1)}, ...), condition=%wide.region_12.12_spmd.clone, body=%wide.region_10.11_spmd.clone.sunk | while | flops 170475264 | bytes 10032288 | solution.py:219
  753.1 34.9 %fusion.30 = f32[2048,11264]{1,0:T(8,128)} fusion(bf16[256,2048]{1,0:T(8,128)(2,1)S(1)} %copy-done.14, bf16[256,5632]{1,0:T(8,128)(2,1)} %get-tuple-element.429, bf16[256,5632]{1,0:T(8,128)(2,1)} %get-tuple-element.430), kind=kOutput, calls=%fused_computation.55 | convolution fusion | flops 11822694400 | bytes 99090432 | tf_op jit(solution)/shard_map/dot_general | solution.py:39
  791.9 15.6 reduce-scatter.10.cloned.1.call-done
  832.5 21.7 fusion.54
  856.1 983.4 %all-reduce.9.cloned.1.call-done = f32[2048,11264]{1,0:T(8,128)} async-done(((f32[2048,11264]{1,0:T(8,128)}), f32[2048,11264]{1,0:T(8,128)}) %all-reduce.9.cloned.1.call-update) | async-done | bytes 92274704
  1850.0 35.5 %reduce-scatter.14.cloned.1.call-done = f32[256,256]{1,0:T(8,128)} async-done(((f32[2048,256]{1,0:T(8,128)}), f32[256,256]{1,0:T(8,128)}) %reduce-scatter.14.cloned.1.call-update) | async-done | bytes 262160 | tf_op jit(solution)/shard_map/reduce_scatter | solution.py:266
  1885.5 45.0 %reduce-scatter.16.cloned.1.call-done = f32[256,256]{1,0:T(8,128)} async-done(((f32[2048,256]{1,0:T(8,128)}), f32[256,256]{1,0:T(8,128)}) %reduce-scatter.16.cloned.1.call-update) | async-done | bytes 262160 | tf_op jit(solution)/shard_map/reduce_scatter | solution.py:267
  1930.4 119.9 %reduce-scatter.12.cloned.1.call-done = f32[256,2048]{1,0:T(8,128)} async-done(((f32[2048,2048]{1,0:T(8,128)}), f32[256,2048]{1,0:T(8,128)}) %reduce-scatter.12.cloned.1.call-update) | async-done | bytes 2097168 | tf_op jit(solution)/shard_map/reduce_scatter | solution.py:265
  2050.4 119.8 %reduce-scatter.18.cloned.1.call-done = f32[256,2048]{1,0:T(8,128)} async-done(((f32[2048,2048]{1,0:T(8,128)}), f32[256,2048]{1,0:T(8,128)}) %reduce-scatter.18.cloned.1.call-update) | async-done | bytes 2097168 | tf_op jit(solution)/shard_map/reduce_scatter | solution.py:268
  2170.2 268.2 %reduce-scatter.20.cloned.1.call-done = f32[704,2048]{1,0:T(8,128)} async-done(((f32[5632,2048]{1,0:T(8,128)}), f32[704,2048]{1,0:T(8,128)}) %reduce-scatter.20.cloned.1.call-update) | async-done | bytes 5767184 | tf_op jit(solution)/shard_map/reduce_scatter | solution.py:179
  2444.7 13.5 fusion.43
  2461.9 24.6 all-reduce.3
  2486.6 13.0 all-reduce.4
  2503.1 676.1 %all-reduce.11.cloned.1.call-done = (f32[256,2048]{1,0:T(8,128)}, f32[256,256]{1,0:T(8,128)}, f32[256,256]{1,0:T(8,128)}, f32[256,2048]{1,0:T(8,128)}, f32[256,5...) async-done(((f32[256,2048]{1,0:T(8,128)}, f32[256,256]{1,0:T(8,128)}, f32[256,256]{1,0:T(8,128)}, f32[256,2048]{1,0:T(8,128)}, f32[256,5632]{1,0:T(8,128)}, ...) | async-done | bytes 22020112 | tf_op jit(solution)/shard_map/psum | solution.py:272
  (714 shorter events, 407.2 us)
Async XLA Ops:
  7.2 29.0 all-gather.12.cloned.1.call-start
  7.9 53.7 %all-gather.14.cloned.1.call-start = ((), (), s32[]{:S(2)}) async-start(), calls=%async_computation.9 | async-start | bytes 1179648 | tf_op jit(solution)/shard_map/all_gather | solution.py:87
  8.7 109.2 %all-gather.10.cloned.1.call-start = ((), (), s32[]{:S(2)}) async-start(), calls=%async_computation.7 | async-start | bytes 9437184 | tf_op jit(solution)/shard_map/all_gather | solution.py:85
  9.4 196.1 %all-gather.16.cloned.1.call-start = ((), (), s32[]{:S(2)}) async-start(), calls=%async_computation.10 | async-start | bytes 9437184 | tf_op jit(solution)/shard_map/all_gather | solution.py:88
  10.0 282.4 %all-gather.18.cloned.1.call-start = ((), (), s32[]{:S(2)}) async-start(), calls=%async_computation.11 | async-start | bytes 25952256 | tf_op jit(solution)/shard_map/all_gather | solution.py:148
  10.6 400.0 %all-gather.20.cloned.1.call-start = ((), (), s32[]{:S(2)}) async-start(), calls=%async_computation.12 | async-start | bytes 25952256 | tf_op jit(solution)/shard_map/all_gather | solution.py:149
  11.1 12.3 copy-start
  11.2 12.7 copy-start.31
  11.2 12.7 copy-start.32
  11.2 12.9 copy-start.34
  11.2 517.8 %all-gather.22.cloned.1.call-start = ((), (), s32[]{:S(2)}) async-start(), calls=%async_computation.13 | async-start | bytes 25952256 | tf_op jit(solution)/shard_map/all_gather | solution.py:158
  11.9 776.2 %reduce-scatter.8.cloned.1.call-start = ((), (), s32[]{:S(2)}) async-start(), calls=%async_computation.14 | async-start | bytes 1310720 | tf_op jit(solution)/shard_map/reduce_scatter | solution.py:230
  23.5 106.8 %copy-start.26 = (f32[8,1,256]{2,1,0:T(1,128)}, f32[8,1,256]{2,1,0:T(1,128)S(1)}, u32[]{:S(2)}) copy-start(f32[8,1,256]{2,1,0:T(1,128)S(1)} %convert_element_type.151) | copy-start | bytes 24580
  23.8 106.4 %copy-start.28 = (f32[256]{0:T(256)}, f32[256]{0:T(256)S(1)}, u32[]{:S(2)}) copy-start(f32[256]{0:T(256)S(1)} %add_rsqrt_fusion.1) | copy-start | bytes 3076
  33.1 103.0 %copy-start.22 = (f32[256,32]{0,1:T(8,128)}, f32[256,32]{0,1:T(8,128)S(1)}, u32[]{:S(2)}) copy-start(f32[256,32]{0,1:T(8,128)S(1)} %get-tuple-element.440) | copy-start | bytes 98308
  33.1 103.0 %copy-start.24 = (f32[256,32]{0,1:T(8,128)}, f32[256,32]{0,1:T(8,128)S(1)}, u32[]{:S(2)}) copy-start(f32[256,32]{0,1:T(8,128)S(1)} %get-tuple-element.441) | copy-start | bytes 98308
  212.7 361.3 %copy-start.4 = (f32[256,2048]{1,0:T(8,128)}, f32[256,2048]{1,0:T(8,128)S(1)}, u32[]{:S(2)}) copy-start(f32[256,2048]{1,0:T(8,128)S(1)} %get-tuple-element.443) | copy-start | bytes 6291460
  212.9 197.7 %copy-start.13 = (bf16[256,2048]{1,0:T(8,128)(2,1)}, bf16[256,2048]{1,0:T(8,128)(2,1)S(1)}, u32[]{:S(2)}) copy-start(bf16[256,2048]{1,0:T(8,128)(2,1)S(1)} %multiply_convert_fusion.4) | copy-start | bytes 3145732
  560.0 14.0 copy-start.17
  751.9 55.5 %reduce-scatter.10.cloned.1.call-start = ((), (), s32[]{:S(2)}) async-start(), calls=%async_computation.15 | async-start | bytes 1310720 | tf_op jit(solution)/shard_map/reduce_scatter | solution.py:231
  752.6 1087.0 %all-reduce.9.cloned.1.call-start = ((), (), s32[]{:S(2)}) async-start(), calls=%async_computation.21 | async-start | bytes 184549376
  788.1 1097.4 %reduce-scatter.14.cloned.1.call-start = ((), (), s32[]{:S(2)}) async-start(), calls=%async_computation.17 | async-start | bytes 2359296 | tf_op jit(solution)/shard_map/reduce_scatter | solution.py:266
  791.8 19.0 copy-start.18
  791.8 1138.6 %reduce-scatter.16.cloned.1.call-start = ((), (), s32[]{:S(2)}) async-start(), calls=%async_computation.18 | async-start | bytes 2359296 | tf_op jit(solution)/shard_map/reduce_scatter | solution.py:267
  810.3 1240.1 %reduce-scatter.12.cloned.1.call-start = ((), (), s32[]{:S(2)}) async-start(), calls=%async_computation.16 | async-start | bytes 18874368 | tf_op jit(solution)/shard_map/reduce_scatter | solution.py:265
  821.2 1349.0 %reduce-scatter.18.cloned.1.call-start = ((), (), s32[]{:S(2)}) async-start(), calls=%async_computation.19 | async-start | bytes 18874368 | tf_op jit(solution)/shard_map/reduce_scatter | solution.py:268
  832.5 1605.9 %reduce-scatter.20.cloned.1.call-start = ((), (), s32[]{:S(2)}) async-start(), calls=%async_computation.20 | async-start | bytes 51904512 | tf_op jit(solution)/shard_map/reduce_scatter | solution.py:179
  854.3 2324.9 %all-reduce.11.cloned.1.call-start = ((), (), s32[]{:S(2)}) async-start(), calls=%async_computation.22 | async-start | bytes 44040192 | tf_op jit(solution)/shard_map/psum | solution.py:272
  2444.7 13.5 copy-start.16
  3179.2 7.0 copy-start.19
  3179.2 8.3 copy-start.9
  3187.5 7.5 slice-start
  (59 other events, 102.5 us)
Sparse Core Ops, SparseCore 0:
  9.9 26.2 all-gather.11
  38.1 23.4 all-gather.13
  63.5 54.3 all-gather.9
  119.6 54.3 all-gather.15
  175.8 116.4 all-gather.17
  294.1 116.4 all-gather.19
  412.5 116.4 all-gather.21
  752.0 27.1 reduce-scatter.7
  781.6 25.7 reduce-scatter.9
  811.1 1028.4 all-reduce.8
  1843.8 41.6 reduce-scatter.13
  1889.2 41.1 reduce-scatter.15
  1934.4 115.9 reduce-scatter.11
  2054.2 115.9 reduce-scatter.17
  2174.1 264.2 reduce-scatter.19
  2442.3 736.8 all-reduce.10
where the time goes:
time: 3210 us
  waiting for transfers between devices  2600 us (81%)
  matrix products  349 us (11%)
  local copies, waits for them, and re-layouts  110 us (3%)
  blocking collectives  89.4 us (3%)
  other arithmetic  33.1 us (1%)
    unnamed x17, waiting for transfers between devices  989 us
    psum x1, waiting for transfers between devices, shards(): lax.psum((gain_one_shard, query_shard, key_shard, value_shard, out_shard,...  676 us
    reduce_scatter x1, waiting for transfers between devices, shards(): lax.psum_scatter(contract_rows(activated, grad_branch), 'fsdp', scatter_d...  268 us
    dot_general x103, matrix products, times_transpose(): lax.dot_general(left, right, (((1,), (1,)), ((), ())), preferred_element_...  128 us
    dot_general x70, matrix products, contract_rows(): lax.dot_general(left, right, (((0,), (0,)), ((), ())), preferred_element_...  124 us
    reduce_scatter x1, waiting for transfers between devices, shards(): lax.psum_scatter(query_term, 'fsdp', scatter_dimension=0, tiled=True)  120 us
    reduce_scatter x1, waiting for transfers between devices, shards(): lax.psum_scatter(out_term, 'fsdp', scatter_dimension=0, tiled=True)  120 us
    all_gather x1, waiting for transfers between devices, shards(): up_piece = lax.all_gather(w_up, 'fsdp', axis=0, tiled=True)  105 us
  transfers between devices with their start and end apart: 16, of which 14 were waited for; matrix products, arithmetic and copies ran while one was open for 7% of the time, Pallas kernels for 0%

commit v1 on v0

--- a/solution.py
+++ b/solution.py
@@ -2,12 +2,38 @@
 import jax.numpy as jnp
 from jax import lax
 from jax.sharding import PartitionSpec as P
+from jax.lax import axis_index, axis_size, ppermute
 
 HEADS = 32
 KV_HEADS = 4
 HEAD_DIM = 64
 EPS = 1e-05
 THETA = 10000.0
+
+
+def make_columns_on_mesh(packet, on_dim):
+    r1 = list(packet.shape[1:])
+    r1[on_dim] *= packet.shape[0]
+    finding = jnp.moveaxis(packet, 0, on_dim).reshape(r1)
+    return finding
+
+
+def entries_render(tile_in, axis_id):
+    t1 = axis_size(axis_id)
+    seen_now = axis_index(axis_id)
+    out_arr, outcome_arr = (t1, seen_now)
+    piece_out, spare = (tile_in[None], 1)
+    while spare < out_arr:
+        base_arr = range(out_arr)
+        x_now = map(lambda at: (at, at ^ spare), base_arr)
+        v_next = list(x_now)
+        mid_arr = ppermute(piece_out, axis_name=axis_id, perm=v_next)
+        taken_in = outcome_arr & spare == 0
+        clean = jnp.where(taken_in, piece_out, mid_arr)
+        placed = jnp.where(taken_in, mid_arr, piece_out)
+        piece_out = jnp.concatenate([clean, placed])
+        spare *= 2
+    return piece_out
 
 
 def rope_tables(positions):
@@ -153,10 +179,14 @@
     sigmoid_gate = jax.nn.sigmoid(gate_sum)
     silu_gate = gate_sum * sigmoid_gate
     activated = (silu_gate * up_sum).astype(jnp.bfloat16)
+
+    def _return_all_numbers(arr, x_in, out_dim=0):
+        passed = entries_render(arr, x_in)
+        w2 = make_columns_on_mesh(passed, out_dim)
+        return w2
+
     branch_out = jnp.dot(
-        activated,
-        lax.all_gather(w_down, "fsdp", axis=0, tiled=True),
-        preferred_element_type=jnp.float32,
+        activated, _return_all_numbers(w_down, "fsdp"), preferred_element_type=jnp.float32
     )
     layer_out = (hidden_one + branch_out).astype(jnp.bfloat16)
     grad_branch = cotangent.astype(jnp.bfloat16)

time: 3210 us -> 3340 us (1.040)
  other arithmetic: 33.1 us -> 86.1 us
  waiting for transfers between devices: 2600 us -> 2650 us
    psum x1, waiting for transfers between devices: 676 us -> 379 us  [shards(): lax.psum((gain_one_shard, query_shard, key_shard, value_shard, out_shard,...]
    ppermute x0 -> x3, waiting for transfers between devices: none -> 254 us  [entries_render(): mid_arr = ppermute(piece_out, axis_name=axis_id, perm=v_next)]
    unnamed x17, waiting for transfers between devices: 989 us -> 1100 us
  transfers between devices with their start and end apart: 16 -> 19, of which waited for: 14 -> 16; matrix products, arithmetic and copies ran while one was open for 7% -> 10% of each run, Pallas kernels for 0% -> 0%
where the time goes in v1:
time: 3340 us; the launch traced here: 3330 us
  waiting for transfers between devices  2650 us (79%)
  matrix products  380 us (11%)
  local copies, waits for them, and re-layouts  103 us (3%)
  blocking collectives  88.8 us (3%)
  other arithmetic  86.1 us (3%)
    unnamed x17, waiting for transfers between devices  1100 us
    psum x1, waiting for transfers between devices, shards(): lax.psum((gain_one_shard, query_shard, key_shard, value_shard, out_shard,...  379 us
    reduce_scatter x1, waiting for transfers between devices, shards(): lax.psum_scatter(contract_rows(activated, grad_branch), 'fsdp', scatter_d...  268 us
    ppermute x3, waiting for transfers between devices, entries_render(): mid_arr = ppermute(piece_out, axis_name=axis_id, perm=v_next)  254 us
    dot_general x103, matrix products, times_transpose(): lax.dot_general(left, right, (((1,), (1,)), ((), ())), preferred_element_...  127 us
    dot_general x70, matrix products, contract_rows(): lax.dot_general(left, right, (((0,), (0,)), ((), ())), preferred_element_...  124 us
    reduce_scatter x1, waiting for transfers between devices, shards(): lax.psum_scatter(query_term, 'fsdp', scatter_dimension=0, tiled=True)  120 us
    reduce_scatter x1, waiting for transfers between devices, shards(): lax.psum_scatter(out_term, 'fsdp', scatter_dimension=0, tiled=True)  120 us
  transfers between devices with their start and end apart: 19, of which 16 were waited for; matrix products, arithmetic and copies ran while one was open for 10% of the time, Pallas kernels for 0%

profile of v1, /device:TPU:0, one launch (start us, length us, event | category | flops | bytes accessed | tf_op | source)
XLA Modules:
  0.0 3328.3 jit_solution(6152382535046860093)
XLA Ops:
  38.2 16.1 all_gather.44
  63.3 16.6 all_gather.46
  81.4 36.5 %all-gather.10.cloned.1.call-done = bf16[2048,2048]{1,0:T(8,128)(2,1)} async-done(((bf16[256,2048]{1,0:T(8,128)(2,1)}), bf16[2048,2048]{1,0:T(8,128)(2,1)}) %all-gather.10.cloned.1.call-update) | async-done | bytes 8388624 | tf_op jit(solution)/shard_map/all_gather | solution.py:111
  144.7 81.6 %while.64 = (s32[]{:T(128)}, bf16[4,8,256,64]{2,3,1,0:T(8,128)(2,1)S(1)}, f32[4,8,256]{2,1,0:T(8,128)S(1)}, bf16[4,8,256,64]{3,2,1,0:T(8,128)(2,1)}, bf16[4,1024...) while((s32[]{:T(128)}, ...), condition=%wide.region_6.7_spmd.clone.clone, body=%wide.region_1.6_spmd.clone.sunk.clone | while | flops 69467904 | bytes 5799230 | solution.py:166
  147.8 17.2 while.63
  168.2 17.2 while.63
  188.7 17.1 while.63
  209.0 17.2 while.63
  235.2 57.0 %all-gather.18.cloned.1.call-done = bf16[2048,5632]{1,0:T(8,128)(2,1)} async-done(((bf16[256,5632]{1,0:T(8,128)(2,1)}), bf16[2048,5632]{1,0:T(8,128)(2,1)}) %all-gather.18.cloned.1.call-update) | async-done | bytes 23068688 | tf_op jit(solution)/shard_map/all_gather | solution.py:174
  305.7 104.8 %all-gather.20.cloned.1.call-done = bf16[2048,5632]{1,0:T(8,128)(2,1)} async-done(((bf16[256,5632]{1,0:T(8,128)(2,1)}), bf16[2048,5632]{1,0:T(8,128)(2,1)}) %all-gather.20.cloned.1.call-update) | async-done | bytes 23068688 | tf_op jit(solution)/shard_map/all_gather | solution.py:175
  424.1 104.7 %all-gather.22.cloned.1.call-done = bf16[5632,2048]{1,0:T(8,128)(2,1)} async-done(((bf16[704,2048]{1,0:T(8,128)(2,1)}), bf16[5632,2048]{1,0:T(8,128)(2,1)}) %all-gather.22.cloned.1.call-update) | async-done | bytes 23068688 | tf_op jit(solution)/shard_map/all_gather | solution.py:194
  528.9 18.5 multiply_convert_fusion.1
  559.9 14.0 multiply_reduce_fusion.1
  584.5 169.9 %while.66 = (s32[]{:T(128)}, f32[4,8,256,64]{2,3,1,0:T(8,128)}, f32[4,1024,64]{1,2,0:T(8,128)}, f32[4,1024,64]{1,2,0:T(8,128)}, bf16[4,8,256,64]{3,2,1,0:T(8,128...) while((s32[]{:T(128)}, f32[4,8,256,64]{2,3,1,0:T(8,128)}, ...), condition=%wide.region_13.14_spmd.clone.clone, body=%wide.region_9.13_spmd.clone.sunk.clone | while | flops 170737408 | bytes 14510505 | solution.py:254
  589.8 34.4 %while.65 = (s32[]{:T(128)}, f32[1024,64]{0,1:T(8,128)S(1)}, f32[1024,64]{0,1:T(8,128)S(1)}, f32[8,256,64]{1,2,0:T(8,128)}, bf16[8,256,64]{2,1,0:T(8,128)(2,1)},...) while((s32[]{:T(128)}, f32[1024,64]{0,1:T(8,128)S(1)}, ...), condition=%wide.region_12.12_spmd.clone, body=%wide.region_10.11_spmd.clone.sunk | while | flops 170475264 | bytes 10032288 | solution.py:249
  632.3 34.4 %while.65 = (s32[]{:T(128)}, f32[1024,64]{0,1:T(8,128)S(1)}, f32[1024,64]{0,1:T(8,128)S(1)}, f32[8,256,64]{1,2,0:T(8,128)}, bf16[8,256,64]{2,1,0:T(8,128)(2,1)},...) while((s32[]{:T(128)}, f32[1024,64]{0,1:T(8,128)S(1)}, ...), condition=%wide.region_12.12_spmd.clone, body=%wide.region_10.11_spmd.clone.sunk | while | flops 170475264 | bytes 10032288 | solution.py:249
  674.8 34.4 %while.65 = (s32[]{:T(128)}, f32[1024,64]{0,1:T(8,128)S(1)}, f32[1024,64]{0,1:T(8,128)S(1)}, f32[8,256,64]{1,2,0:T(8,128)}, bf16[8,256,64]{2,1,0:T(8,128)(2,1)},...) while((s32[]{:T(128)}, f32[1024,64]{0,1:T(8,128)S(1)}, ...), condition=%wide.region_12.12_spmd.clone, body=%wide.region_10.11_spmd.clone.sunk | while | flops 170475264 | bytes 10032288 | solution.py:249
  717.3 34.4 %while.65 = (s32[]{:T(128)}, f32[1024,64]{0,1:T(8,128)S(1)}, f32[1024,64]{0,1:T(8,128)S(1)}, f32[8,256,64]{1,2,0:T(8,128)}, bf16[8,256,64]{2,1,0:T(8,128)(2,1)},...) while((s32[]{:T(128)}, f32[1024,64]{0,1:T(8,128)S(1)}, ...), condition=%wide.region_12.12_spmd.clone, body=%wide.region_10.11_spmd.clone.sunk | while | flops 170475264 | bytes 10032288 | solution.py:249
  755.2 35.1 %fusion.30 = f32[2048,11264]{1,0:T(8,128)} fusion(bf16[256,2048]{1,0:T(8,128)(2,1)} %copy-done.14, bf16[256,5632]{1,0:T(8,128)(2,1)} %get-tuple-element.431, bf16[256,5632]{1,0:T(8,128)(2,1)} %get-tuple-element.432), kind=kOutput, calls=%fused_computation.60 | convolution fusion | flops 11822694400 | bytes 99090432 | tf_op jit(solution)/shard_map/dot_general | solution.py:65
  794.2 15.8 reduce-scatter.10.cloned.1.call-done
  835.1 21.7 fusion.54
  873.1 1092.6 %all-reduce.9.cloned.1.call-done = f32[2048,11264]{1,0:T(8,128)} async-done(((f32[2048,11264]{1,0:T(8,128)}), f32[2048,11264]{1,0:T(8,128)}) %all-reduce.9.cloned.1.call-update) | async-done | bytes 92274704
  1976.0 35.6 %reduce-scatter.14.cloned.1.call-done = f32[256,256]{1,0:T(8,128)} async-done(((f32[2048,256]{1,0:T(8,128)}), f32[256,256]{1,0:T(8,128)}) %reduce-scatter.14.cloned.1.call-update) | async-done | bytes 262160 | tf_op jit(solution)/shard_map/reduce_scatter | solution.py:296
  2011.6 44.4 %reduce-scatter.16.cloned.1.call-done = f32[256,256]{1,0:T(8,128)} async-done(((f32[2048,256]{1,0:T(8,128)}), f32[256,256]{1,0:T(8,128)}) %reduce-scatter.16.cloned.1.call-update) | async-done | bytes 262160 | tf_op jit(solution)/shard_map/reduce_scatter | solution.py:297
  2056.0 119.9 %reduce-scatter.12.cloned.1.call-done = f32[256,2048]{1,0:T(8,128)} async-done(((f32[2048,2048]{1,0:T(8,128)}), f32[256,2048]{1,0:T(8,128)}) %reduce-scatter.12.cloned.1.call-update) | async-done | bytes 2097168 | tf_op jit(solution)/shard_map/reduce_scatter | solution.py:295
  2175.9 119.8 %reduce-scatter.18.cloned.1.call-done = f32[256,2048]{1,0:T(8,128)} async-done(((f32[2048,2048]{1,0:T(8,128)}), f32[256,2048]{1,0:T(8,128)}) %reduce-scatter.18.cloned.1.call-update) | async-done | bytes 2097168 | tf_op jit(solution)/shard_map/reduce_scatter | solution.py:298
  2295.7 268.2 %reduce-scatter.20.cloned.1.call-done = f32[704,2048]{1,0:T(8,128)} async-done(((f32[5632,2048]{1,0:T(8,128)}), f32[704,2048]{1,0:T(8,128)}) %reduce-scatter.20.cloned.1.call-update) | async-done | bytes 5767184 | tf_op jit(solution)/shard_map/reduce_scatter | solution.py:209
  2578.8 248.5 %collective-permute-done.2 = bf16[4,704,2048]{2,1,0:T(8,128)(2,1)} collective-permute-done((bf16[4,704,2048]{2,1,0:T(8,128)(2,1)}, bf16[4,704,2048]{2,1,0:T(8,128)(2,1)}, u32[]{:S(2)}, u32[]{:S(2)}) %collective-permute-start.2) | collective-permute-done | bytes 11534368 | tf_op jit(solution)/shard_map/ppermute | solution.py:30
  2827.3 16.0 broadcast_select_fusion.1
  2843.4 19.9 pad_maximum_fusion
  2885.3 23.9 all-reduce.3
  2925.9 378.9 %all-reduce.11.cloned.1.call-done = (f32[256,2048]{1,0:T(8,128)}, f32[256,256]{1,0:T(8,128)}, f32[256,256]{1,0:T(8,128)}, f32[256,2048]{1,0:T(8,128)}, f32[256,5...) async-done(((f32[256,2048]{1,0:T(8,128)}, f32[256,256]{1,0:T(8,128)}, f32[256,256]{1,0:T(8,128)}, f32[256,2048]{1,0:T(8,128)}, f32[256,5632]{1,0:T(8,128)}, ...) | async-done | bytes 22020112 | tf_op jit(solution)/shard_map/psum | solution.py:302
  (658 shorter events, 501.5 us)
Async XLA Ops:
  7.2 28.9 all-gather.12.cloned.1.call-start
  7.9 53.6 %all-gather.14.cloned.1.call-start = ((), (), s32[]{:S(2)}) async-start(), calls=%async_computation.9 | async-start | bytes 1179648 | tf_op jit(solution)/shard_map/all_gather | solution.py:113
  8.7 109.2 %all-gather.10.cloned.1.call-start = ((), (), s32[]{:S(2)}) async-start(), calls=%async_computation.7 | async-start | bytes 9437184 | tf_op jit(solution)/shard_map/all_gather | solution.py:111
  9.4 217.0 %all-gather.16.cloned.1.call-start = ((), (), s32[]{:S(2)}) async-start(), calls=%async_computation.10 | async-start | bytes 9437184 | tf_op jit(solution)/shard_map/all_gather | solution.py:114
  10.0 282.3 %all-gather.18.cloned.1.call-start = ((), (), s32[]{:S(2)}) async-start(), calls=%async_computation.11 | async-start | bytes 25952256 | tf_op jit(solution)/shard_map/all_gather | solution.py:174
  10.6 12.0 copy-start
  10.6 399.9 %all-gather.20.cloned.1.call-start = ((), (), s32[]{:S(2)}) async-start(), calls=%async_computation.12 | async-start | bytes 25952256 | tf_op jit(solution)/shard_map/all_gather | solution.py:175
  11.2 11.7 copy-start.35
  11.2 11.9 copy-start.37
  11.2 517.7 %all-gather.22.cloned.1.call-start = ((), (), s32[]{:S(2)}) async-start(), calls=%async_computation.13 | async-start | bytes 25952256 | tf_op jit(solution)/shard_map/all_gather | solution.py:194
  11.9 778.5 %reduce-scatter.8.cloned.1.call-start = ((), (), s32[]{:S(2)}) async-start(), calls=%async_computation.14 | async-start | bytes 1310720 | tf_op jit(solution)/shard_map/reduce_scatter | solution.py:260
  22.6 107.7 %copy-start.27 = (f32[8,1,256]{2,1,0:T(1,128)}, f32[8,1,256]{2,1,0:T(1,128)S(1)}, u32[]{:S(2)}) copy-start(f32[8,1,256]{2,1,0:T(1,128)S(1)} %convert_element_type.151) | copy-start | bytes 24580
  22.9 107.4 %copy-start.31 = (f32[256]{0:T(256)}, f32[256]{0:T(256)S(1)}, u32[]{:S(2)}) copy-start(f32[256]{0:T(256)S(1)} %add_rsqrt_fusion.1) | copy-start | bytes 3076
  32.2 104.1 %copy-start.23 = (f32[256,32]{0,1:T(8,128)}, f32[256,32]{0,1:T(8,128)S(1)}, u32[]{:S(2)}) copy-start(f32[256,32]{0,1:T(8,128)S(1)} %get-tuple-element.446) | copy-start | bytes 98308
  32.2 104.1 %copy-start.25 = (f32[256,32]{0,1:T(8,128)}, f32[256,32]{0,1:T(8,128)S(1)}, u32[]{:S(2)}) copy-start(f32[256,32]{0,1:T(8,128)S(1)} %get-tuple-element.447) | copy-start | bytes 98308
  235.0 339.0 %copy-start.8 = (f32[256,2048]{1,0:T(8,128)}, f32[256,2048]{1,0:T(8,128)S(1)}, u32[]{:S(2)}) copy-start(f32[256,2048]{1,0:T(8,128)S(1)} %get-tuple-element.449) | copy-start | bytes 6291460
  235.2 175.3 %copy-start.14 = (bf16[256,2048]{1,0:T(8,128)(2,1)}, bf16[256,2048]{1,0:T(8,128)(2,1)S(1)}, u32[]{:S(2)}) copy-start(bf16[256,2048]{1,0:T(8,128)(2,1)S(1)} %multiply_convert_fusion.4) | copy-start | bytes 3145732
  559.9 14.0 copy-start.18
  754.4 55.5 %reduce-scatter.10.cloned.1.call-start = ((), (), s32[]{:S(2)}) async-start(), calls=%async_computation.15 | async-start | bytes 1310720 | tf_op jit(solution)/shard_map/reduce_scatter | solution.py:261
  755.2 1210.5 %all-reduce.9.cloned.1.call-start = ((), (), s32[]{:S(2)}) async-start(), calls=%async_computation.21 | async-start | bytes 184549376
  790.4 1221.2 %reduce-scatter.14.cloned.1.call-start = ((), (), s32[]{:S(2)}) async-start(), calls=%async_computation.17 | async-start | bytes 2359296 | tf_op jit(solution)/shard_map/reduce_scatter | solution.py:296
  794.1 19.2 copy-start.19
  794.1 1261.9 %reduce-scatter.16.cloned.1.call-start = ((), (), s32[]{:S(2)}) async-start(), calls=%async_computation.18 | async-start | bytes 2359296 | tf_op jit(solution)/shard_map/reduce_scatter | solution.py:297
  812.9 1363.1 %reduce-scatter.12.cloned.1.call-start = ((), (), s32[]{:S(2)}) async-start(), calls=%async_computation.16 | async-start | bytes 18874368 | tf_op jit(solution)/shard_map/reduce_scatter | solution.py:295
  823.8 1471.9 %reduce-scatter.18.cloned.1.call-start = ((), (), s32[]{:S(2)}) async-start(), calls=%async_computation.19 | async-start | bytes 18874368 | tf_op jit(solution)/shard_map/reduce_scatter | solution.py:298
  835.0 1728.9 %reduce-scatter.20.cloned.1.call-start = ((), (), s32[]{:S(2)}) async-start(), calls=%async_computation.20 | async-start | bytes 51904512 | tf_op jit(solution)/shard_map/reduce_scatter | solution.py:209
  856.8 2447.9 %all-reduce.11.cloned.1.call-start = ((), (), s32[]{:S(2)}) async-start(), calls=%async_computation.22 | async-start | bytes 44040192 | tf_op jit(solution)/shard_map/psum | solution.py:302
  857.1 5.7 collective-permute-start
  870.2 1693.8 %collective-permute-start.1 = (bf16[2,704,2048]{2,1,0:T(8,128)(2,1)}, bf16[2,704,2048]{2,1,0:T(8,128)(2,1)}, u32[]{:S(2)}, u32[]{:S(2)}) collective-permute-start(bf16[2,704,2048]{2,1,0:T(8,128)(2,1)} %pad_maximum_fusion.2), channel_id=1, source_target_pairs={{0,2},{1,3},{2,0},{3,1},{4,6},{5,7},{6,4},{7,5},{8,10},{9,11},{10,... | collective-permute-start | bytes 17301512 | tf_op jit(solution)/shard_map/ppermute | solution.py:30
  2577.4 249.9 %collective-permute-start.2 = (bf16[4,704,2048]{2,1,0:T(8,128)(2,1)}, bf16[4,704,2048]{2,1,0:T(8,128)(2,1)}, u32[]{:S(2)}, u32[]{:S(2)}) collective-permute-start(bf16[4,704,2048]{2,1,0:T(8,128)(2,1)} %pad_maximum_fusion.1), channel_id=1, source_target_pairs={{0,4},{1,5},{2,6},{3,7},{4,0},{5,1},{6,2},{7,3},{8,12},{9,13},{10,... | collective-permute-start | bytes 34603016 | tf_op jit(solution)/shard_map/ppermute | solution.py:30
  2843.4 19.9 copy-start.16
  2869.3 12.4 copy-start.17
  (28 other events, 104.5 us)
Sparse Core Ops, SparseCore 0:
  9.9 26.1 all-gather.11
  38.0 23.4 all-gather.13
  63.4 54.3 all-gather.9
  119.6 54.3 all-gather.15
  175.7 116.4 all-gather.17
  294.0 116.4 all-gather.19
  412.4 116.4 all-gather.21
  754.6 27.1 reduce-scatter.7
  784.1 25.7 reduce-scatter.9
  813.6 1152.0 all-reduce.8
  1969.9 41.6 reduce-scatter.13
  2014.7 41.1 reduce-scatter.15
  2060.0 115.9 reduce-scatter.11
  2179.8 115.9 reduce-scatter.17
  2299.6 264.2 reduce-scatter.19
  2567.8 736.8 all-reduce.10
